TPU v7x, 32 devices: a whole 2x2x4 slice. The times are simulated.
32 devices in a mesh: groups: 2 (over y), tile: 4 (over z), pair: 2 (over x), sub: 2 (over core).
Axes of the slice: x: 2, y: 2, z: 4, core: 2. Of those that a mesh axis runs over, the one named last changes fastest.
Arguments:
- ref_chips: bfloat16 [4, 256, 4096], P(('groups', 'pair'), ('tile', 'sub')), parts along dimension 0, may hold values from -300 to 700
- search_windows: bfloat16 [4, 512, 16384], P(('groups', 'pair'), ('tile', 'sub')), parts along dimension 0, may hold values from -300 to 700
- dest_block: int32 [4, 512, 1], P(('groups', 'pair'), ('tile', 'sub')), parts along dimension 0, may hold values from 0 to 7; in each aligned block of 64 rows (0 to 63, 64 to 127, ..., all dimensions but the last counted through in order) at most 16 rows name the same one
- dest_slot: int32 [4, 512], P(('groups', 'pair'), ('tile', 'sub')), parts along dimension 0, may hold values from 0 to 31
Outputs:
- smoothed_scores: float32 [4, 256, 4096], P(('groups', 'pair'), ('tile', 'sub')), parts along dimension 0
There are 2 independent parts, one for each index of `groups`. A program takes and returns all parts, laid end to end along the dimension named above; each array names one. Nothing has to cross between parts.
Inputs may be any that keep to these rules, and one draw needn't show every extreme that they name: `dest_block`: in the rows of one device (aligned blocks of 64 windows), no block index is named by more than 16 windows.
All inputs are finite; a program needn't handle non-finite values.
Results may differ from a plain program's by a relative error of at most 0.0003.
Values may be sent and summed in bfloat16 or wider, within the bound.
No kernel may reach another device: no remote copies, remote signals or barrier semaphores. Data moves between devices by JAX's collectives and lax.ppermute only.
A program may use at most 64 MiB of HBM per device.

v0:
```python
import math
import jax
import jax.numpy as jnp
from jax import lax
from jax.sharding import PartitionSpec as P

CHIP = 64
WIN = 128
GC = 8
precise = lax.Precision.HIGHEST
epsilon = 1e-06


def padded(block, sides, width):
    for axis, dim in sides:
        count = lax.axis_size(axis)
        forward = [(i, i + 1) for i in range(count - 1)]
        backward = [(target, source) for source, target in forward]
        low = lax.ppermute(
            lax.slice_in_dim(block, block.shape[dim] - width, None, axis=dim), axis, forward
        )
        high = lax.ppermute(lax.slice_in_dim(block, 0, width, axis=dim), axis, backward)
        block = jnp.concatenate([low, block, high], axis=dim)
    return block


def tables(length, width):
    freqs = jnp.arange(length, dtype=jnp.int32)[:, None]
    places = jnp.arange(width, dtype=jnp.int32)[None, :]
    phase = freqs * places % length
    angle = phase.astype(jnp.float32) * (2.0 * math.pi / length)
    return (jnp.cos(angle), jnp.sin(angle))


def spectrum(image, cosine, sine_table):
    first_real = jnp.einsum("kn,bnm->bkm", cosine, image, precision=precise)
    first_imag = -jnp.einsum("kn,bnm->bkm", sine_table, image, precision=precise)
    spec_real = jnp.einsum("bkm,lm->bkl", first_real, cosine, precision=precise) + jnp.einsum(
        "bkm,lm->bkl", first_imag, sine_table, precision=precise
    )
    spec_imag = jnp.einsum("bkm,lm->bkl", first_imag, cosine, precision=precise) - jnp.einsum(
        "bkm,lm->bkl", first_real, sine_table, precision=precise
    )
    return (spec_real, spec_imag)


def centre(chips_raw, chip_side):
    chip_float = chips_raw.astype(jnp.float32).reshape(-1, chip_side, chip_side)
    centred = chip_float - jnp.mean(chip_float, axis=(1, 2), keepdims=True)
    chip_std = jnp.sqrt(jnp.mean(centred * centred, axis=(1, 2)) + epsilon)
    return (centred, chip_std)


def match(chip_real, chip_imag, chip_std, windows_raw, chip_side, window_side):
    offsets = window_side - chip_side
    cos_full, sin_full = tables(window_side, window_side)
    cos_part = cos_full[:offsets]
    sin_part = sin_full[:offsets]
    window_float = windows_raw.astype(jnp.float32).reshape(-1, window_side, window_side)
    win_real, win_imag = spectrum(window_float, cos_full, sin_full)
    product_real = chip_real * win_real + chip_imag * win_imag
    product_imag = chip_real * win_imag - chip_imag * win_real
    half_real = jnp.einsum("ak,bkl->bal", cos_part, product_real, precision=precise) - jnp.einsum(
        "ak,bkl->bal", sin_part, product_imag, precision=precise
    )
    half_imag = jnp.einsum("ak,bkl->bal", cos_part, product_imag, precision=precise) + jnp.einsum(
        "ak,bkl->bal", sin_part, product_real, precision=precise
    )
    numerator = (
        jnp.einsum("bal,el->bae", half_real, cos_part, precision=precise)
        - jnp.einsum("bal,el->bae", half_imag, sin_part, precision=precise)
    ) / (window_side * window_side)
    starts = jnp.arange(offsets, dtype=jnp.int32)[:, None]
    pixels = jnp.arange(window_side, dtype=jnp.int32)[None, :]
    window_band = ((pixels >= starts) & (pixels < starts + chip_side)).astype(jnp.float32)
    first_rows = jnp.einsum("ax,bxy->bay", window_band, window_float, precision=precise)
    first_sum = jnp.einsum("bay,ey->bae", first_rows, window_band, precision=precise)
    second_rows = jnp.einsum(
        "ax,bxy->bay", window_band, window_float * window_float, precision=precise
    )
    second_sum = jnp.einsum("bay,ey->bae", second_rows, window_band, precision=precise)
    patch_mean = first_sum / (chip_side * chip_side)
    patch_var = second_sum / (chip_side * chip_side) - patch_mean * patch_mean
    score = numerator / (chip_side * chip_std[:, None, None] * jnp.sqrt(patch_var + epsilon))
    return score.reshape(-1, offsets * offsets)


def in_blocks(function, operands):
    amount = operands[0].shape[0]
    block_rows = 16
    shaped = tuple(
        (item.reshape((amount // block_rows, block_rows) + item.shape[1:]) for item in operands)
    )
    result = lax.map(lambda grouped: function(*grouped), shaped)
    return result.reshape(amount, -1)


def on_device(ref_chips, search_windows, dest_block, dest_slot):
    chips = ref_chips[0]
    windows = search_windows[0]
    targets = dest_block[0, :, 0]
    target_slot = dest_slot[0]
    chip_side = CHIP
    window_side = WIN
    offsets = window_side - chip_side
    window_amount = windows.shape[0]
    chip_amount = chips.shape[0]
    devices = lax.axis_size(("tile", "sub"))
    capacity = max(2, 2 * window_amount // devices)
    slot_amount = devices * capacity
    order = jnp.arange(window_amount, dtype=jnp.int32)
    matches = targets[:, None] == targets[None, :]
    earlier = order[:, None] > order[None, :]
    ranking = jnp.sum((matches & earlier).astype(jnp.int32), axis=1)
    positions = targets * capacity + ranking
    slot_buffer = jnp.full((slot_amount,), -1, jnp.int32).at[positions].set(target_slot)
    cos_chip, sin_chip = tables(window_side, chip_side)
    requests = slot_buffer.reshape(devices, capacity)
    found = jnp.take(
        chips,
        jnp.maximum(
            lax.all_to_all(requests, ("tile", "sub"), split_axis=0, concat_axis=0, tiled=True), 0
        ),
        axis=0,
    )
    fetched = lax.all_to_all(found, ("tile", "sub"), split_axis=0, concat_axis=0, tiled=True)
    own_chips = jnp.take(fetched.reshape(slot_amount, chip_side * chip_side), positions, axis=0)

    def match_own(chip_part, window_part):
        centred_part, std_part = centre(chip_part, chip_side)
        real_part, imag_part = spectrum(centred_part, cos_chip, sin_chip)
        return match(real_part, imag_part, std_part, window_part, chip_side, window_side)

    own_scores = in_blocks(match_own, (own_chips, windows))
    score_buffer = (
        jnp.zeros((slot_amount, offsets * offsets), jnp.float32).at[positions].set(own_scores)
    )
    scores, slots_here = (
        lax.all_to_all(score_buffer, ("tile", "sub"), split_axis=0, concat_axis=0, tiled=True),
        lax.all_to_all(slot_buffer, ("tile", "sub"), split_axis=0, concat_axis=0, tiled=True),
    )
    hits_table = (slots_here[None, :] == jnp.arange(chip_amount, dtype=jnp.int32)[:, None]).astype(
        jnp.float32
    )
    total = jnp.dot(hits_table, scores, precision=precise)
    looks = jnp.sum(hits_table, axis=1)
    average = total / jnp.maximum(looks, 1.0)[:, None]
    grid = average.reshape(-1, GC, offsets * offsets)
    extended = padded(grid, ((("tile", "sub"), 0),), 1)
    vertical = extended[:-2] + extended[2:]
    sideways = jnp.pad(grid, ((0, 0), (1, 1), (0, 0)))
    horizontal = sideways[:, :-2] + sideways[:, 2:]
    smoothed = (4.0 * grid + vertical + horizontal) / 8.0
    return smoothed.reshape(1, chip_amount, offsets * offsets)


def solution(mesh):
    return jax.shard_map(
        on_device,
        mesh=mesh,
        in_specs=(
            P(("groups", "pair"), ("tile", "sub"), None),
            P(("groups", "pair"), ("tile", "sub"), None),
            P(("groups", "pair"), ("tile", "sub"), None),
            P(("groups", "pair"), ("tile", "sub")),
        ),
        out_specs=P(("groups", "pair"), ("tile", "sub"), None),
        check_vma=False,
    )
```

profile of v0, /device:TPU:1, one launch (start us, length us, event | category | flops | bytes accessed | tf_op | source)
XLA Modules:
  0.0 226.2 jit_solution(14719844709658617581)
XLA Ops:
  2.6 11.0 %all_to_all.35 = s32[8,1,16]{2,1,0:T(1,128)S(1)} all-to-all(s32[8,1,16]{2,1,0:T(1,128)S(1)} %bitcast.236), channel_id=1, replica_groups=mesh['groups'=2,'tile'=4,'pair'=2,'sub'=2] {'tile','sub'}, dimensions={0} | all-to-all | bytes 1024 | tf_op jit(solution)/shard_map/all_to_all | solution.py:122
  16.1 4.2 %all-to-all-start.2 = ((bf16[8,16,4096]{2,1,0:T(8,128)(2,1)}), bf16[8,16,4096]{2,1,0:T(8,128)(2,1)S(1)}, u32[]{:S(2)}, u32[]{:S(2)}) async-start(bf16[8,16,4096]{2,1,0:T(8,128)(2,1)} %broadcast_select_fusion), calls=%async_computation.2 | async-start | bytes 2097152 | tf_op jit(solution)/shard_map/all_to_all | solution.py:126
  21.1 24.7 %all-to-all-done.2 = bf16[8,16,4096]{2,1,0:T(8,128)(2,1)S(1)} async-done(((bf16[8,16,4096]{2,1,0:T(8,128)(2,1)}), bf16[8,16,4096]{2,1,0:T(8,128)(2,1)S(1)}, u32[]{:S(2)}, u32[]{:S(2)}) %all-to-all-start.2) | async-done | bytes 1048608 | tf_op jit(solution)/shard_map/all_to_all | solution.py:126
  45.9 4.2 %all-to-all-start = ((s32[8,16,1]{1,2,0:T(1,128)}), s32[8,16,1]{1,2,0:T(1,128)S(1)}, u32[]{:S(2)}, u32[]{:S(2)}) async-start(s32[8,16,1]{1,2,0:T(1,128)} %bitcast.5), calls=%async_computation | async-start | bytes 8192 | tf_op jit(solution)/shard_map/all_to_all | solution.py:140
  51.0 109.2 %while.14 = (s32[]{:T(128)}, f32[4,16,4096]{2,1,0:T(8,128)S(1)}, bf16[4,16,4096]{2,1,0:T(8,128)(2,1)S(1)}, bf16[4,16,16384]{2,1,0:T(8,128)(2,1)}, s32[]{:T(128)}) while((s32[]{:T(128)}, f32[4,16,4096]{2,1,0:T(8,128)S(1)}, bf16[4,16,4096]{2,1,0:T(8,128)(2,1)S(1)}, bf16[4,16,16384]{2,1,0:T(8,128)(2,1)}, s32[]{:T(128)}) %tuple.39), condition=%wide.region_5.6_spmd.clone.clone, body=%wide.region_2.5_spmd.clone.clone.sunk | while | flops 4872994816 | bytes 46598104 | solution.py:94
  58.1 2.0 fusion.248
  60.1 1.9 convolution_add_fusion.5
  62.1 1.9 fusion.252
  64.0 1.9 convolution_subtract_fusion.5
  85.4 2.0 fusion.248
  87.4 1.9 convolution_add_fusion.5
  89.3 1.9 fusion.252
  91.3 1.9 convolution_subtract_fusion.5
  112.7 2.0 fusion.248
  114.6 1.9 convolution_add_fusion.5
  118.5 1.9 convolution_subtract_fusion.5
  139.9 2.0 fusion.248
  141.9 1.9 convolution_add_fusion.5
  145.8 1.9 convolution_subtract_fusion.5
  160.3 2.6 %scatter_custom_fusion.1 = f32[128,4096]{1,0:T(8,128)} fusion(s32[64]{0:T(128)S(1)} %fusion.136, f32[64,4096]{1,0:T(8,128)S(1)} %bitcast.237, f32[]{:T(128)} %constant.141.clone.1), kind=kCustom, calls=%fused_computation.150 | custom fusion | bytes 2097156 | tf_op jit(solution)/shard_map/scatter | solution.py:136
  162.9 5.1 %all-to-all-start.3 = ((f32[8,16,4096]{2,1,0:T(8,128)}), f32[8,16,4096]{2,1,0:T(8,128)S(1)}, u32[]{:S(2)}, u32[]{:S(2)}) async-start(f32[8,16,4096]{2,1,0:T(8,128)} %bitcast.15), calls=%async_computation.3 | async-start | bytes 4194304 | tf_op jit(solution)/shard_map/all_to_all | solution.py:139
  169.4 46.7 %all-to-all-done.3 = f32[8,16,4096]{2,1,0:T(8,128)S(1)} async-done(((f32[8,16,4096]{2,1,0:T(8,128)}), f32[8,16,4096]{2,1,0:T(8,128)S(1)}, u32[]{:S(2)}, u32[]{:S(2)}) %all-to-all-start.3) | async-done | bytes 2097184 | tf_op jit(solution)/shard_map/all_to_all | solution.py:139
  218.9 2.4 %collective-permute-start.1 = (f32[1,8,4096]{2,1,0:T(8,128)S(1)}, f32[1,8,4096]{2,1,0:T(8,128)S(1)}, u32[]{:S(2)}, u32[]{:S(2)}) collective-permute-start(f32[1,8,4096]{2,1,0:T(8,128)S(1)} %get-tuple-element.139), channel_id=1, source_target_pairs={{1,0},{4,1},{5,4},{8,5},{9,8},{12,9},{13,12},{3,2},{6,3},{7,6},{10... | collective-permute-start | bytes 393224 | tf_op jit(solution)/shard_map/ppermute | solution.py:22
  221.3 3.9 %collective-permute-done.1 = f32[1,8,4096]{2,1,0:T(8,128)S(1)} collective-permute-done((f32[1,8,4096]{2,1,0:T(8,128)S(1)}, f32[1,8,4096]{2,1,0:T(8,128)S(1)}, u32[]{:S(2)}, u32[]{:S(2)}) %collective-permute-start.1) | collective-permute-done | bytes 131104 | tf_op jit(solution)/shard_map/ppermute | solution.py:22
  (164 shorter events, 92.8 us)
Async XLA Ops:
  0.0 13.7 %copy-start = (bf16[1,32,4096]{2,1,0:T(8,128)(2,1)S(1)}, bf16[1,32,4096]{2,1,0:T(8,128)(2,1)}, u32[]{:S(2)}) copy-start(bf16[1,32,4096]{2,1,0:T(8,128)(2,1)} %param.6) | copy-start | bytes 786436
  14.9 6.1 %copy-start.1 = (s32[1,64,1]{1,2,0:T(1,128)S(1)}, s32[1,64,1]{1,2,0:T(1,128)}, u32[]{:S(2)}) copy-start(s32[1,64,1]{1,2,0:T(1,128)} %param.8) | copy-start | bytes 772
  16.1 29.8 %all-to-all-start.2 = ((bf16[8,16,4096]{2,1,0:T(8,128)(2,1)}), bf16[8,16,4096]{2,1,0:T(8,128)(2,1)S(1)}, u32[]{:S(2)}, u32[]{:S(2)}) async-start(bf16[8,16,4096]{2,1,0:T(8,128)(2,1)} %broadcast_select_fusion), calls=%async_computation.2 | async-start | bytes 2097152 | tf_op jit(solution)/shard_map/all_to_all | solution.py:126
  45.9 117.0 %all-to-all-start = ((s32[8,16,1]{1,2,0:T(1,128)}), s32[8,16,1]{1,2,0:T(1,128)S(1)}, u32[]{:S(2)}, u32[]{:S(2)}) async-start(s32[8,16,1]{1,2,0:T(1,128)} %bitcast.5), calls=%async_computation | async-start | bytes 8192 | tf_op jit(solution)/shard_map/all_to_all | solution.py:140
  162.9 53.2 %all-to-all-start.3 = ((f32[8,16,4096]{2,1,0:T(8,128)}), f32[8,16,4096]{2,1,0:T(8,128)S(1)}, u32[]{:S(2)}, u32[]{:S(2)}) async-start(f32[8,16,4096]{2,1,0:T(8,128)} %bitcast.15), calls=%async_computation.3 | async-start | bytes 4194304 | tf_op jit(solution)/shard_map/all_to_all | solution.py:139
  217.0 4.3 %collective-permute-start = (f32[1,8,4096]{2,1,0:T(8,128)S(1)}, f32[1,8,4096]{2,1,0:T(8,128)S(1)}, u32[]{:S(2)}, u32[]{:S(2)}) collective-permute-start(f32[1,8,4096]{2,1,0:T(8,128)S(1)} %get-tuple-element.138), channel_id=1, source_target_pairs={{0,1},{1,4},{4,5},{5,8},{8,9},{9,12},{12,13},{2,3},{3,6},{6,7},{7,... | collective-permute-start | bytes 393224 | tf_op jit(solution)/shard_map/ppermute | solution.py:19
  218.9 6.3 %collective-permute-start.1 = (f32[1,8,4096]{2,1,0:T(8,128)S(1)}, f32[1,8,4096]{2,1,0:T(8,128)S(1)}, u32[]{:S(2)}, u32[]{:S(2)}) collective-permute-start(f32[1,8,4096]{2,1,0:T(8,128)S(1)} %get-tuple-element.139), channel_id=1, source_target_pairs={{1,0},{4,1},{5,4},{8,5},{9,8},{12,9},{13,12},{3,2},{6,3},{7,6},{10... | collective-permute-start | bytes 393224 | tf_op jit(solution)/shard_map/ppermute | solution.py:22
where the time goes:
time: 227 us; the launch traced here: 226 us
  matrix products  98 us (43%)
  waiting for transfers between devices  75.3 us (33%)
  starting transfers between devices  17.8 us (8%)
  local copies, waits for them, and re-layouts  14.4 us (6%)
  blocking collectives  11 us (5%)
  other arithmetic  8.43 us (4%)
    all_to_all x1, waiting for transfers between devices, on_device(): lax.all_to_all(score_buffer, ('tile', 'sub'), split_axis=0, concat_axis=0...  46.7 us
    all_to_all x1, waiting for transfers between devices, on_device(): lax.all_to_all(found, ('tile', 'sub'), split_axis=0, concat_axis=0, tiled...  24.7 us
    dot_general x8, matrix products, spectrum(): jnp.einsum('bkm,lm->bkl', first_real, sine_table, precision=precise)  15.5 us
    dot_general x8, matrix products, spectrum(): jnp.einsum('bkm,lm->bkl', first_real, cosine, precision=precise)  15.1 us
    dot_general x8, matrix products, spectrum(): jnp.einsum('bkm,lm->bkl', first_imag, sine_table, precision=precise)  15.1 us
    dot_general x8, matrix products, spectrum(): jnp.einsum('bkm,lm->bkl', first_imag, cosine, precision=precise)  15 us
    all_to_all x1, blocking collectives, on_device(): lax.all_to_all(requests, ('tile', 'sub'), split_axis=0, concat_axis=0, ti...  11 us
    dot_general x8, matrix products, spectrum(): first_real = jnp.einsum('kn,bnm->bkm', cosine, image, precision=precise)  6.31 us
  transfers between devices with their start and end apart: 5, of which 3 were waited for; matrix products, arithmetic and copies ran while one was open for 50% of the time, Pallas kernels for 0%

commit v1 on v0

--- a/solution.py
+++ b/solution.py
@@ -9,6 +9,30 @@
 GC = 8
 precise = lax.Precision.HIGHEST
 epsilon = 1e-06
+
+
+def split_up(x, dim, size):
+    shape = x.shape
+    blocks = x.reshape(*shape[:dim], size, shape[dim] // size, *shape[dim + 1 :])
+    return jnp.moveaxis(blocks, dim, 0)
+
+
+def joined_along(blocks, dim):
+    shape = list(blocks.shape[1:])
+    shape[dim] *= blocks.shape[0]
+    return jnp.moveaxis(blocks, 0, dim).reshape(shape)
+
+
+def exchange_directly(value, axis, split_dim, concat_dim):
+    size, here = (lax.axis_size(axis), lax.axis_index(axis))
+    blocks = split_up(value, split_dim, size)
+    out = blocks
+    for step in range(1, size):
+        target, source = ((here + step) % size, (here - step) % size)
+        sent = lax.dynamic_index_in_dim(blocks, target, 0)
+        partner_block = lax.ppermute(sent, axis, [(i, (i + step) % size) for i in range(size)])
+        out = lax.dynamic_update_slice_in_dim(out, partner_block, source, axis=0)
+    return joined_along(out, concat_dim)
 
 
 def padded(block, sides, width):
@@ -123,7 +147,7 @@
         ),
         axis=0,
     )
-    fetched = lax.all_to_all(found, ("tile", "sub"), split_axis=0, concat_axis=0, tiled=True)
+    fetched = exchange_directly(found, ("tile", "sub"), 0, 0)
     own_chips = jnp.take(fetched.reshape(slot_amount, chip_side * chip_side), positions, axis=0)
 
     def match_own(chip_part, window_part):

time: 227 us -> 224 us (0.987)
  starting transfers between devices: 17.8 us -> 35.1 us
  blocking collectives: 11 us -> 0 us
  waiting for transfers between devices: 75.3 us -> 65.6 us
    all_to_all x1, waiting for transfers between devices: 24.7 us -> 3.28 us  [on_device(): lax.all_to_all(requests, ('tile', 'sub'), split_axis=0, concat_axis=0, ti...]
    ppermute x0 -> x7, starting transfers between devices: none -> 15.6 us  [exchange_directly(): lax.ppermute(sent, axis, [(i, (i + step) % size) for i in range(size)])]
    ppermute x0 -> x7, waiting for transfers between devices: none -> 11.7 us  [exchange_directly(): lax.ppermute(sent, axis, [(i, (i + step) % size) for i in range(size)])]
    all_to_all x1 -> x0, blocking collectives: 11 us -> none  [on_device(): lax.all_to_all(requests, ('tile', 'sub'), split_axis=0, concat_axis=0, ti...]
  transfers between devices with their start and end apart: 5 -> 12, of which waited for: 3 -> 5; matrix products, arithmetic and copies ran while one was open for 50% -> 52% of each run, Pallas kernels for 0% -> 0%
where the time goes in v1:
time: 224 us
  matrix products  98 us (44%)
  waiting for transfers between devices  65.6 us (29%)
  starting transfers between devices  35.1 us (16%)
  local copies, waits for them, and re-layouts  15.1 us (7%)
  other arithmetic  8.25 us (4%)
    all_to_all x1, waiting for transfers between devices, on_device(): lax.all_to_all(score_buffer, ('tile', 'sub'), split_axis=0, concat_axis=0...  46.7 us
    ppermute x7, starting transfers between devices, exchange_directly(): lax.ppermute(sent, axis, [(i, (i + step) % size) for i in range(size)])  15.6 us
    dot_general x8, matrix products, spectrum(): jnp.einsum('bkm,lm->bkl', first_real, sine_table, precision=precise)  15.5 us
    dot_general x8, matrix products, spectrum(): jnp.einsum('bkm,lm->bkl', first_real, cosine, precision=precise)  15.1 us
    dot_general x8, matrix products, spectrum(): jnp.einsum('bkm,lm->bkl', first_imag, sine_table, precision=precise)  15.1 us
    dot_general x8, matrix products, spectrum(): jnp.einsum('bkm,lm->bkl', first_imag, cosine, precision=precise)  15 us
    ppermute x7, waiting for transfers between devices, exchange_directly(): lax.ppermute(sent, axis, [(i, (i + step) % size) for i in range(size)])  11.7 us
    all_to_all x1, starting transfers between devices, on_device(): lax.all_to_all(requests, ('tile', 'sub'), split_axis=0, concat_axis=0, ti...  6.37 us
  transfers between devices with their start and end apart: 12, of which 5 were waited for; matrix products, arithmetic and copies ran while one was open for 52% of the time, Pallas kernels for 0%

profile of v1, /device:TPU:1, one launch (start us, length us, event | category | flops | bytes accessed | tf_op | source)
XLA Modules:
  0.0 223.7 jit_solution(16707251174720662178)
XLA Ops:
  3.2 6.4 %all-to-all-start.1 = ((s32[8,1,16]{2,1,0:T(1,128)}), s32[8,1,16]{2,1,0:T(1,128)S(1)}, u32[]{:S(2)}, u32[]{:S(2)}) async-start(s32[8,1,16]{2,1,0:T(1,128)} %bitcast.6), calls=%async_computation.1 | async-start | bytes 8192 | tf_op jit(solution)/shard_map/all_to_all | solution.py:146
  11.1 3.3 %all-to-all-done.1 = s32[8,1,16]{2,1,0:T(1,128)S(1)} async-done(((s32[8,1,16]{2,1,0:T(1,128)}), s32[8,1,16]{2,1,0:T(1,128)S(1)}, u32[]{:S(2)}, u32[]{:S(2)}) %all-to-all-start.1) | async-done | bytes 544 | tf_op jit(solution)/shard_map/all_to_all | solution.py:146
  14.3 3.9 %all-to-all-start = ((s32[8,16,1]{1,2,0:T(1,128)}), s32[8,16,1]{1,2,0:T(1,128)S(1)}, u32[]{:S(2)}, u32[]{:S(2)}) async-start(s32[8,16,1]{1,2,0:T(1,128)} %bitcast.5), calls=%async_computation | async-start | bytes 8192 | tf_op jit(solution)/shard_map/all_to_all | solution.py:164
  21.7 2.0 collective-permute-start.5
  23.8 2.1 collective-permute-start.4
  27.0 9.8 %collective-permute-done.1 = bf16[1,1,16,4096]{3,2,0,1:T(8,128)(2,1)S(1)} collective-permute-done((bf16[1,1,16,4096]{3,2,0,1:T(8,128)(2,1)S(1)}, bf16[1,1,16,4096]{3,2,0,1:T(8,128)(2,1)S(1)}, u32[]{:S(2)}, u32[]{:S(2)}) %collective-permute-start.1) | collective-permute-done | bytes 131104 | tf_op jit(solution)/shard_map/ppermute | solution.py:33
  36.8 8.5 %collective-permute-start.2 = (bf16[1,1,16,4096]{3,2,0,1:T(8,128)(2,1)S(1)}, bf16[1,1,16,4096]{3,2,0,1:T(8,128)(2,1)S(1)}, u32[]{:S(2)}, u32[]{:S(2)}) collective-permute-start(bf16[1,1,16,4096]{3,2,0,1:T(8,128)(2,1)S(1)} %get-tuple-element.142), channel_id=1, source_target_pairs={{0,5},{1,8},{4,9},{5,12},{8,13},{9,0},{12,1},{13,4},{2,7},{3,10},{... | collective-permute-start | bytes 393224 | tf_op jit(solution)/shard_map/ppermute | solution.py:33
  48.4 109.4 %while.14 = (s32[]{:T(128)}, f32[4,16,4096]{2,1,0:T(8,128)S(1)}, bf16[4,16,4096]{2,1,0:T(8,128)(2,1)S(1)}, bf16[4,16,16384]{2,1,0:T(8,128)(2,1)}, s32[]{:T(128)}) while((s32[]{:T(128)}, f32[4,16,4096]{2,1,0:T(8,128)S(1)}, bf16[4,16,4096]{2,1,0:T(8,128)(2,1)S(1)}, bf16[4,16,16384]{2,1,0:T(8,128)(2,1)}, s32[]{:T(128)}) %tuple.45), condition=%wide.region_5.6_spmd.clone.clone, body=%wide.region_2.5_spmd.clone.clone.sunk | while | flops 4872994816 | bytes 46598104 | solution.py:118
  55.7 2.0 fusion.248
  57.7 1.9 convolution_add_fusion.5
  61.6 1.9 convolution_subtract_fusion.5
  83.0 2.0 fusion.248
  84.9 1.9 convolution_add_fusion.5
  88.8 1.9 convolution_subtract_fusion.5
  110.2 2.0 fusion.248
  112.2 1.9 convolution_add_fusion.5
  116.1 1.9 convolution_subtract_fusion.5
  137.5 2.0 fusion.248
  139.4 1.9 convolution_add_fusion.5
  157.9 2.6 %scatter_custom_fusion.1 = f32[128,4096]{1,0:T(8,128)} fusion(s32[64]{0:T(128)S(1)} %fusion.136, f32[64,4096]{1,0:T(8,128)S(1)} %bitcast.252, f32[]{:T(128)} %constant.239.clone.1), kind=kCustom, calls=%fused_computation.150 | custom fusion | bytes 2097156 | tf_op jit(solution)/shard_map/scatter | solution.py:160
  160.5 5.0 %all-to-all-start.2 = ((f32[8,16,4096]{2,1,0:T(8,128)}), f32[8,16,4096]{2,1,0:T(8,128)S(1)}, u32[]{:S(2)}, u32[]{:S(2)}) async-start(f32[8,16,4096]{2,1,0:T(8,128)} %bitcast.23), calls=%async_computation.2 | async-start | bytes 4194304 | tf_op jit(solution)/shard_map/all_to_all | solution.py:163
  166.9 46.7 %all-to-all-done.2 = f32[8,16,4096]{2,1,0:T(8,128)S(1)} async-done(((f32[8,16,4096]{2,1,0:T(8,128)}), f32[8,16,4096]{2,1,0:T(8,128)S(1)}, u32[]{:S(2)}, u32[]{:S(2)}) %all-to-all-start.2) | async-done | bytes 2097184 | tf_op jit(solution)/shard_map/all_to_all | solution.py:163
  216.4 2.4 %collective-permute-start.8 = (f32[1,8,4096]{2,1,0:T(8,128)S(1)}, f32[1,8,4096]{2,1,0:T(8,128)S(1)}, u32[]{:S(2)}, u32[]{:S(2)}) collective-permute-start(f32[1,8,4096]{2,1,0:T(8,128)S(1)} %get-tuple-element.146), channel_id=1, source_target_pairs={{1,0},{4,1},{5,4},{8,5},{9,8},{12,9},{13,12},{3,2},{6,3},{7,6},{10... | collective-permute-start | bytes 393224 | tf_op jit(solution)/shard_map/ppermute | solution.py:46
  218.8 3.9 %collective-permute-done.8 = f32[1,8,4096]{2,1,0:T(8,128)S(1)} collective-permute-done((f32[1,8,4096]{2,1,0:T(8,128)S(1)}, f32[1,8,4096]{2,1,0:T(8,128)S(1)}, u32[]{:S(2)}, u32[]{:S(2)}) %collective-permute-start.8) | collective-permute-done | bytes 131104 | tf_op jit(solution)/shard_map/ppermute | solution.py:46
  (184 shorter events, 104.1 us)
Async XLA Ops:
  0.0 18.3 %copy-start = (bf16[1,32,4096]{2,1,0:T(8,128)(2,1)S(1)}, bf16[1,32,4096]{2,1,0:T(8,128)(2,1)}, u32[]{:S(2)}) copy-start(bf16[1,32,4096]{2,1,0:T(8,128)(2,1)} %param.6) | copy-start | bytes 786436
  3.2 11.2 %all-to-all-start.1 = ((s32[8,1,16]{2,1,0:T(1,128)}), s32[8,1,16]{2,1,0:T(1,128)S(1)}, u32[]{:S(2)}, u32[]{:S(2)}) async-start(s32[8,1,16]{2,1,0:T(1,128)} %bitcast.6), calls=%async_computation.1 | async-start | bytes 8192 | tf_op jit(solution)/shard_map/all_to_all | solution.py:146
  14.3 146.1 %all-to-all-start = ((s32[8,16,1]{1,2,0:T(1,128)}), s32[8,16,1]{1,2,0:T(1,128)S(1)}, u32[]{:S(2)}, u32[]{:S(2)}) async-start(s32[8,16,1]{1,2,0:T(1,128)} %bitcast.5), calls=%async_computation | async-start | bytes 8192 | tf_op jit(solution)/shard_map/all_to_all | solution.py:164
  19.8 6.7 %collective-permute-start = (bf16[1,1,16,4096]{3,2,0,1:T(8,128)(2,1)S(1)}, bf16[1,1,16,4096]{3,2,0,1:T(8,128)(2,1)S(1)}, u32[]{:S(2)}, u32[]{:S(2)}) collective-permute-start(bf16[1,1,16,4096]{3,2,0,1:T(8,128)(2,1)S(1)} %get-tuple-element.144), channel_id=1, source_target_pairs={{0,1},{1,4},{4,5},{5,8},{8,9},{9,12},{12,13},{13,0},{2,3},{3,6},{6... | collective-permute-start | bytes 393224 | tf_op jit(solution)/shard_map/ppermute | solution.py:33
  21.6 25.8 %collective-permute-start.6 = (bf16[1,1,16,4096]{3,2,0,1:T(8,128)(2,1)S(1)}, bf16[1,1,16,4096]{3,2,0,1:T(8,128)(2,1)S(1)}, u32[]{:S(2)}, u32[]{:S(2)}) collective-permute-start(bf16[1,1,16,4096]{3,2,0,1:T(8,128)(2,1)S(1)} %get-tuple-element.138), channel_id=1, source_target_pairs={{0,13},{1,0},{4,1},{5,4},{8,5},{9,8},{12,9},{13,12},{2,15},{3,2},{... | collective-permute-start | bytes 393224 | tf_op jit(solution)/shard_map/ppermute | solution.py:33
  21.7 25.7 %collective-permute-start.5 = (bf16[1,1,16,4096]{3,2,0,1:T(8,128)(2,1)S(1)}, bf16[1,1,16,4096]{3,2,0,1:T(8,128)(2,1)S(1)}, u32[]{:S(2)}, u32[]{:S(2)}) collective-permute-start(bf16[1,1,16,4096]{3,2,0,1:T(8,128)(2,1)S(1)} %get-tuple-element.139), channel_id=1, source_target_pairs={{0,12},{1,13},{4,0},{5,1},{8,4},{9,5},{12,8},{13,9},{2,14},{3,15},... | collective-permute-start | bytes 393224 | tf_op jit(solution)/shard_map/ppermute | solution.py:33
  23.8 23.6 %collective-permute-start.4 = (bf16[1,1,16,4096]{3,2,0,1:T(8,128)(2,1)S(1)}, bf16[1,1,16,4096]{3,2,0,1:T(8,128)(2,1)S(1)}, u32[]{:S(2)}, u32[]{:S(2)}) collective-permute-start(bf16[1,1,16,4096]{3,2,0,1:T(8,128)(2,1)S(1)} %get-tuple-element.140), channel_id=1, source_target_pairs={{0,9},{1,12},{4,13},{5,0},{8,1},{9,4},{12,5},{13,8},{2,11},{3,14},... | collective-permute-start | bytes 393224 | tf_op jit(solution)/shard_map/ppermute | solution.py:33
  25.8 21.5 %collective-permute-start.3 = (bf16[1,1,16,4096]{3,2,0,1:T(8,128)(2,1)S(1)}, bf16[1,1,16,4096]{3,2,0,1:T(8,128)(2,1)S(1)}, u32[]{:S(2)}, u32[]{:S(2)}) collective-permute-start(bf16[1,1,16,4096]{3,2,0,1:T(8,128)(2,1)S(1)} %get-tuple-element.141), channel_id=1, source_target_pairs={{0,8},{1,9},{4,12},{5,13},{8,0},{9,1},{12,4},{13,5},{2,10},{3,11},... | collective-permute-start | bytes 393224 | tf_op jit(solution)/shard_map/ppermute | solution.py:33
  26.5 10.3 %collective-permute-start.1 = (bf16[1,1,16,4096]{3,2,0,1:T(8,128)(2,1)S(1)}, bf16[1,1,16,4096]{3,2,0,1:T(8,128)(2,1)S(1)}, u32[]{:S(2)}, u32[]{:S(2)}) collective-permute-start(bf16[1,1,16,4096]{3,2,0,1:T(8,128)(2,1)S(1)} %get-tuple-element.143), channel_id=1, source_target_pairs={{0,4},{1,5},{4,8},{5,9},{8,12},{9,13},{12,0},{13,1},{2,6},{3,7},{6... | collective-permute-start | bytes 393224 | tf_op jit(solution)/shard_map/ppermute | solution.py:33
  36.8 10.5 %collective-permute-start.2 = (bf16[1,1,16,4096]{3,2,0,1:T(8,128)(2,1)S(1)}, bf16[1,1,16,4096]{3,2,0,1:T(8,128)(2,1)S(1)}, u32[]{:S(2)}, u32[]{:S(2)}) collective-permute-start(bf16[1,1,16,4096]{3,2,0,1:T(8,128)(2,1)S(1)} %get-tuple-element.142), channel_id=1, source_target_pairs={{0,5},{1,8},{4,9},{5,12},{8,13},{9,0},{12,1},{13,4},{2,7},{3,10},{... | collective-permute-start | bytes 393224 | tf_op jit(solution)/shard_map/ppermute | solution.py:33
  160.5 53.1 %all-to-all-start.2 = ((f32[8,16,4096]{2,1,0:T(8,128)}), f32[8,16,4096]{2,1,0:T(8,128)S(1)}, u32[]{:S(2)}, u32[]{:S(2)}) async-start(f32[8,16,4096]{2,1,0:T(8,128)} %bitcast.23), calls=%async_computation.2 | async-start | bytes 4194304 | tf_op jit(solution)/shard_map/all_to_all | solution.py:163
  214.5 4.3 %collective-permute-start.7 = (f32[1,8,4096]{2,1,0:T(8,128)S(1)}, f32[1,8,4096]{2,1,0:T(8,128)S(1)}, u32[]{:S(2)}, u32[]{:S(2)}) collective-permute-start(f32[1,8,4096]{2,1,0:T(8,128)S(1)} %get-tuple-element.145), channel_id=1, source_target_pairs={{0,1},{1,4},{4,5},{5,8},{8,9},{9,12},{12,13},{2,3},{3,6},{6,7},{7,... | collective-permute-start | bytes 393224 | tf_op jit(solution)/shard_map/ppermute | solution.py:43
  216.4 6.3 %collective-permute-start.8 = (f32[1,8,4096]{2,1,0:T(8,128)S(1)}, f32[1,8,4096]{2,1,0:T(8,128)S(1)}, u32[]{:S(2)}, u32[]{:S(2)}) collective-permute-start(f32[1,8,4096]{2,1,0:T(8,128)S(1)} %get-tuple-element.146), channel_id=1, source_target_pairs={{1,0},{4,1},{5,4},{8,5},{9,8},{12,9},{13,12},{3,2},{6,3},{7,6},{10... | collective-permute-start | bytes 393224 | tf_op jit(solution)/shard_map/ppermute | solution.py:46
